TPU v7x, 32 devices: a whole 2x2x4 slice. The times are simulated.
32 devices in a mesh: lat: 4 (over y, x), lon: 8 (over z, core).
Axes of the slice: x: 2, y: 2, z: 4, core: 2. Of those that a mesh axis runs over, the one named last changes fastest.
Arguments:
- fine_nodes: float32 [2, 128, 256, 512], P(None, 'lat', 'lon'), may hold values from -6 to 6
- mid_nodes: float32 [2, 32, 64, 512], P(None, 'lat', 'lon'), may hold values from -6 to 6
- coarse_nodes: float32 [2, 8, 16, 512], P(None, 'lat', 'lon'), may hold values from -6 to 6
- edge_flags: int32 [8, 128, 256], P(None, 'lat', 'lon'), may hold values 0 or 1
- proc_weights: bfloat16 [3, 4, 512, 512], replicated, may hold values from -0.25 to 0.25
- bridge_weights: bfloat16 [4, 512, 512], replicated, may hold values from -0.25 to 0.25
- proc_biases: float32 [3, 512], replicated, may hold values from -3 to 3
Outputs:
- refined: float32 [2, 128, 256, 512], P(None, 'lat', 'lon')
- fine_average: bfloat16 [2, 128, 256, 512], P(None, 'lat', 'lon')
All inputs are finite; a program needn't handle non-finite values. No bound on the sum of `edge_flags` on one device may be relied on, other than what follows from the above.
Results may differ from a plain program's by a relative error of at most 0.005.
Values may be sent and summed in bfloat16 or wider, within the bound.
A program may use at most 128 MiB of HBM per device.

v0:
```python
import functools

import jax
import jax.numpy as jnp
import numpy as np
from jax import lax
from jax.experimental import pallas as pl
from jax.experimental.pallas import tpu as pltpu
from jax.sharding import PartitionSpec as P

offsets = ((-1, -1), (-1, 0), (-1, 1), (0, -1), (0, 1), (1, -1), (1, 0), (1, 1))
bf16 = jnp.bfloat16
f32 = jnp.float32
MESH = pl.DeviceIdType.MESH
LANES = 128
EDGE = 16


def mm(a, b):
    return jnp.dot(a, b, preferred_element_type=f32)


def half_silu(u):
    return u * jnp.tanh(u) + u


def silu(x):
    return half_silu(x * 0.5)


def edge_of(step, count):
    if step == 0:
        return list(range(count))
    return [count - 1] if step < 0 else [0]


def small_tables(samples, rows, cols):
    nodes = samples * rows * cols
    padded = -(-nodes // 16) * 16
    pick = np.zeros((8 * EDGE, padded), np.float32)
    slot = {}
    for k, (p, q) in enumerate(offsets):
        e = 0
        for b in range(samples):
            for i in edge_of(p, rows):
                for j in edge_of(q, cols):
                    pick[k * EDGE + e, (b * rows + i) * cols + j] = 1
                    slot[k, b, i, j] = padded + k * EDGE + e
                    e += 1
        assert e <= EDGE
    gather = np.zeros((8, padded, padded + 8 * EDGE), np.float32)
    for k, (p, q) in enumerate(offsets):
        for b in range(samples):
            for i in range(rows):
                for j in range(cols):
                    a, c = i + p, j + q
                    over = (-1 if a < 0 else int(a >= rows), -1 if c < 0 else int(c >= cols))
                    if over == (0, 0):
                        source = (b * rows + a) * cols + c
                    else:
                        source = slot[offsets.index(over), b, a % rows, c % cols]
                    gather[k, (b * rows + i) * cols + j, source] = 1
    return jnp.asarray(pick, bf16), jnp.asarray(gather.reshape(8 * padded, -1), bf16)


def pool_table(rows, cols, out_rows):
    n = np.arange(rows * cols)
    parent = (n // cols // 4) * (cols // 4) + (n % cols) // 4
    return (parent[None, :] == np.arange(out_rows)[:, None]).astype(np.float32)


def sweep_kernel(
    dims,
    x_hbm, mid_ref, coarse_ref, flag_ref, proc_hbm, bridge_hbm, bias_ref,
    pool_ref, place_ref, row_ref, count_ref,
    pick_mid, gather_mid, pick_coarse, gather_coarse, pool_mid, spread_mid,
    one_hbm, avg_hbm, spread_ref,
    recv, shifted, x_buf, one_buf, avg_buf, w, w2h, live_buf, pool_buf,
    out_buf, halo, mid_send, mid_full, coarse_send, coarse_full, mid_hidden, coarse_hidden,
    x_sems, w_sems, one_sems, avg_sems, send_sems, recv_sems,
):
    samples, rows, cols, d, step, mid_dims, coarse_dims = dims
    per = rows // step
    chunk = step * cols
    chunks = samples * per
    lat, lon = lax.axis_index("lat"), lax.axis_index("lon")
    lats, lons = lax.axis_size("lat"), lax.axis_size("lon")
    half = jnp.asarray(0.5, bf16)

    def target(k):
        p, q = offsets[k]
        return (lax.rem(lat - p + lats, lats), lax.rem(lon - q + lons, lons))

    barrier = pltpu.get_barrier_semaphore()
    for k in range(8):
        pl.semaphore_signal(barrier, inc=1, device_id=target(k), device_id_type=MESH)
    copies = [
        pltpu.make_async_copy(x_hbm.at[pl.ds(c * chunk, chunk)], x_buf.at[pl.ds(c * chunk, chunk)], x_sems.at[c])
        for c in range(chunks)
    ]
    loads = [pltpu.make_async_copy(proc_hbm.at[0], w.at[pl.ds(0, 4)], w_sems.at[0])]
    loads += [pltpu.make_async_copy(proc_hbm.at[1], w.at[pl.ds(4, 4)], w_sems.at[1])]
    loads += [pltpu.make_async_copy(proc_hbm.at[2], w.at[pl.ds(8, 4)], w_sems.at[2])]
    loads += [pltpu.make_async_copy(bridge_hbm, w.at[pl.ds(12, 4)], w_sems.at[3])]
    for copy in copies + loads:
        copy.start()

    table = jnp.zeros((rows, 8 * cols), f32)
    for k in range(8):
        table = table + mm(flag_ref[k].astype(bf16), place_ref[k])
    spread_flags = mm(row_ref[...], table.astype(bf16))
    node = lax.broadcasted_iota(jnp.int32, spread_flags.shape, 0)
    lane = lax.broadcasted_iota(jnp.int32, spread_flags.shape, 1)
    own = jnp.where(node % cols == lane % cols, spread_flags, 0.0).astype(bf16)
    live = mm(own, count_ref[...])
    node = lax.broadcasted_iota(jnp.int32, live.shape, 0) // cols
    lane = lax.broadcasted_iota(jnp.int32, live.shape, 1)
    top = jnp.where(lat == 0, 0, -1)
    bottom = jnp.where(lat == lats - 1, rows - 1, -1)
    live_buf[...] = jnp.where(
        ((lane < 3) & (node == top)) | ((lane > 4) & (node == bottom)), 0.0, live
    )

    for copy in copies:
        copy.wait()
    base = {1: 0, 6: samples * cols, 3: 2 * samples * cols, 4: 2 * samples * cols + samples * rows}
    size = {1: samples * cols, 6: samples * cols, 3: samples * rows, 4: samples * rows}
    corner = 2 * samples * (cols + rows)
    for n, k in enumerate((0, 2, 5, 7)):
        base[k], size[k] = corner + n * EDGE, EDGE
    per_sample = rows * cols
    grid_buf = x_buf.reshape(samples * rows, cols, d)
    row16 = lax.broadcasted_iota(jnp.int32, (EDGE, d), 0)
    for k, (p, q) in enumerate(offsets):
        i, j = edge_of(p, rows)[0], edge_of(q, cols)[0]
        if p == 0:
            out_buf[pl.ds(base[k], size[k]), :] = grid_buf[:, j, :].astype(bf16)
        elif q == 0:
            for b in range(samples):
                out_buf[pl.ds(base[k] + b * cols, cols), :] = x_buf[
                    pl.ds(b * per_sample + i * cols, cols), :
                ].astype(bf16)
        else:
            value = jnp.zeros((EDGE, d), f32)
            for b in range(samples):
                at = b * per_sample + i * cols + j
                value = jnp.where(row16 == b, jnp.broadcast_to(x_buf[at : at + 1, :], (EDGE, d)), value)
            out_buf[pl.ds(base[k], EDGE), :] = value.astype(bf16)
    pl.semaphore_wait(barrier, 8)

    def exchange(level, source, dest, spans, shift):
        sends = []
        for k in range(8):
            at, count = spans[k]
            sends.append(
                pltpu.make_async_remote_copy(
                    src_ref=source.at[pl.ds(at, count)],
                    dst_ref=dest.at[pl.ds(shift + at, count)],
                    send_sem=send_sems.at[level * 8 + k],
                    recv_sem=recv_sems.at[level * 8 + k],
                    device_id=target(k),
                    device_id_type=MESH,
                )
            )
        for send in sends:
            send.start()
        return sends

    sends = exchange(0, out_buf, halo, {k: (base[k], size[k]) for k in range(8)}, 0)

    loads[0].wait()
    w2h[0] = w[2] * half
    bias = bias_ref[0:1, :] * 0.5

    def project_body(c, carry):
        window = pl.ds(pl.multiple_of(c * chunk, chunk), chunk)
        xh = x_buf[window, :].astype(bf16) * half
        recv[window, :] = (mm(xh, w[0]) + bias).astype(bf16)
        one_buf[window, :] = mm(xh, w[1])
        return carry

    lax.fori_loop(0, chunks, project_body, 0)
    for send in sends:
        send.wait()
    hs = mm(halo[...] * half, w[1])

    def place(s, low, high, b, top_row, count):
        size = count * cols
        col = lax.broadcasted_iota(jnp.int32, (size, d), 0) % cols
        left = jnp.broadcast_to(low[:, None, :], (count, cols, d)).reshape(size, d)
        right = jnp.broadcast_to(high[:, None, :], (count, cols, d)).reshape(size, d)
        minus = jnp.where(col == 0, left, pltpu.roll(s, 1, 0))
        plus = jnp.where(col == cols - 1, right, pltpu.roll(s, size - 1, 0))
        window = pl.ds(top_row * cols, size)
        shifted[0, b, window, :] = minus.astype(bf16)
        shifted[1, b, window, :] = s.astype(bf16)
        shifted[2, b, window, :] = plus.astype(bf16)

    for b in range(samples):
        for k, row in ((1, 0), (6, rows + 1)):
            at = base[k] + b * cols
            low, high = base[k - 1] + b, base[k + 1] + b
            place(hs[at : at + cols], hs[low : low + 1], hs[high : high + 1], b, row, 1)
    for c in range(chunks):
        b, part = divmod(c, per)
        at = b * rows + part * step
        low, high = base[3] + at, base[4] + at
        place(
            one_buf[pl.ds(c * chunk, chunk), :], hs[low : low + step], hs[high : high + step],
            b, 1 + part * step, step,
        )

    def body(c, carry):
        b = c // per
        part = c % per
        window = pl.ds(pl.multiple_of(c * chunk, chunk), chunk)
        flags = live_buf[pl.ds(pl.multiple_of(part * chunk, chunk), chunk), :]
        r = recv[window, :]
        total = jnp.zeros((chunk, d), f32)
        for k, (p, q) in enumerate(offsets):
            start = pl.multiple_of((part * step + 1 + p) * cols, cols)
            u = r + shifted[q + 1, b, pl.ds(start, chunk), :]
            z = mm(half_silu(u), w2h[0]).astype(bf16)
            on = jnp.broadcast_to(flags[:, k : k + 1], (chunk, LANES)).astype(bf16)
            on = jnp.concatenate([on] * (d // LANES), axis=1)
            total = total + (half_silu(z) * on).astype(f32)
        average = (total * 0.125).astype(bf16)
        avg_buf[window, :] = average
        one = x_buf[window, :] + mm(average, w[3])
        one_buf[window, :] = one
        small = chunk // 16
        pool_buf[pl.ds(pl.multiple_of(c * small, small), small), :] = (
            mm(pool_ref[...], one.astype(bf16)) * (1 / 16)
        ).astype(bf16)
        pltpu.make_async_copy(avg_buf.at[window], avg_hbm.at[window], avg_sems.at[c]).start()
        pltpu.make_async_copy(one_buf.at[window], one_hbm.at[window], one_sems.at[c]).start()
        return carry

    lax.fori_loop(0, chunks, body, 0)

    def small_pass(level, state, level_dims, pick, gather, send, full, hidden):
        _, n_rows, n_cols = level_dims
        padded = state.shape[0]
        xh = state.astype(bf16) * half
        s = mm(xh, w[4 * level + 1]).astype(bf16)
        full[pl.ds(0, padded), :] = s
        send[...] = mm(pick[...], s).astype(bf16)
        moves = exchange(level, send, full, {k: (k * EDGE, EDGE) for k in range(8)}, padded)
        w2h[level] = w[4 * level + 2] * half
        r = mm(xh, w[4 * level]) + bias_ref[level : level + 1, :] * 0.5
        for move in moves:
            move.wait()
        near = mm(gather[...], full[...])
        for k in range(8):
            u = r + near[k * padded : (k + 1) * padded]
            hidden[pl.ds(k * padded, padded), :] = half_silu(u).astype(bf16)
        message = half_silu(mm(hidden[...], w2h[level]))
        row = lax.broadcasted_iota(jnp.int32, (padded, d), 0) // n_cols % n_rows
        first = row == jnp.where(lat == 0, 0, -1)
        last = row == jnp.where(lat == lats - 1, n_rows - 1, -1)
        total = jnp.zeros((padded, d), f32)
        for k, (p, q) in enumerate(offsets):
            part = message[k * padded : (k + 1) * padded]
            if p:
                part = jnp.where(first if p < 0 else last, 0.0, part)
            total = total + part
        return state + mm((total * 0.125).astype(bf16), w[4 * level + 3])

    for load in loads[1:]:
        load.wait()
    mid_zero = mid_ref[...] + silu(mm(pool_buf[...], w[12]))
    mid_one = small_pass(1, mid_zero, mid_dims, pick_mid, gather_mid, mid_send, mid_full, mid_hidden)
    small = (mm(pool_mid[...], mid_one.astype(bf16)) * (1 / 16)).astype(bf16)
    coarse_zero = coarse_ref[...] + silu(mm(small, w[13]))
    coarse_one = small_pass(
        2, coarse_zero, coarse_dims, pick_coarse, gather_coarse, coarse_send, coarse_full, coarse_hidden
    )
    lifted = silu(mm(coarse_one.astype(bf16), w[14])).astype(bf16)
    mid_two = mid_one + mm(spread_mid[...], lifted)
    spread_ref[...] = silu(mm(mid_two.astype(bf16), w[15])).astype(bf16)

    def finish(c, carry):
        window = pl.ds(pl.multiple_of(c * chunk, chunk), chunk)
        pltpu.make_async_copy(avg_buf.at[window], avg_hbm.at[window], avg_sems.at[c]).wait()
        pltpu.make_async_copy(one_buf.at[window], one_hbm.at[window], one_sems.at[c]).wait()
        return carry

    lax.fori_loop(0, chunks, finish, 0)


def add_kernel(one_ref, spread_ref, table_ref, out_ref):
    out_ref[...] = one_ref[...] + mm(table_ref[...], spread_ref[...])


def local(
    fine_nodes, mid_nodes, coarse_nodes, edge_flags, proc_weights, bridge_weights, proc_biases
):
    samples, rows, cols, d = fine_nodes.shape
    mid_dims, coarse_dims = mid_nodes.shape[:3], coarse_nodes.shape[:3]
    step = 8
    chunk = step * cols
    total = samples * rows * cols
    chunks = total // chunk
    mid_count, coarse_count = int(np.prod(mid_dims)), int(np.prod(coarse_dims))
    coarse_padded = -(-coarse_count // 16) * 16
    pick_mid, gather_mid = small_tables(*mid_dims)
    pick_coarse, gather_coarse = small_tables(*coarse_dims)
    pool = pool_table(step, cols, chunk // 16)
    pool_mid = np.zeros((coarse_padded, mid_count), np.float32)
    each, few = mid_count // samples, coarse_count // samples
    for b in range(samples):
        pool_mid[b * few : (b + 1) * few, b * each : (b + 1) * each] = pool_table(*mid_dims[1:], few)
    place = np.zeros((8, cols, 8 * cols), np.float32)
    count = np.zeros((8 * cols, 8), np.float32)
    for k in range(8):
        place[k, np.arange(cols), k * cols + np.arange(cols)] = 1
        count[k * cols : (k + 1) * cols, k] = 1
    row_of = (np.arange(rows * cols)[:, None] // cols == np.arange(rows)[None, :])
    tables = [
        jnp.asarray(t, bf16) for t in (pool, place, row_of.astype(np.float32), count)
    ]
    levels = [
        pick_mid, gather_mid, pick_coarse, gather_coarse,
        jnp.asarray(pool_mid, bf16), jnp.asarray(pool_mid.T, bf16),
    ]
    coarse = jnp.pad(coarse_nodes.reshape(coarse_count, d), ((0, coarse_padded - coarse_count), (0, 0)))
    halo_rows = 2 * samples * (rows + cols) + 4 * EDGE
    vmem = pl.BlockSpec(memory_space=pltpu.VMEM)
    anywhere = pl.BlockSpec(memory_space=pl.ANY)
    dma = pltpu.SemaphoreType.DMA
    one, average, spread = pl.pallas_call(
        functools.partial(sweep_kernel, (samples, rows, cols, d, step, mid_dims, coarse_dims)),
        out_shape=(
            jax.ShapeDtypeStruct((total, d), f32),
            jax.ShapeDtypeStruct((total, d), bf16),
            jax.ShapeDtypeStruct((mid_count, d), bf16),
        ),
        in_specs=[anywhere, vmem, vmem, vmem, anywhere, anywhere, vmem] + [vmem] * 10,
        out_specs=(anywhere, anywhere, vmem),
        scratch_shapes=[
            pltpu.VMEM((total, d), bf16),
            pltpu.VMEM((3, samples, (rows + 2) * cols, d), bf16),
            pltpu.VMEM((total, d), f32),
            pltpu.VMEM((total, d), f32),
            pltpu.VMEM((total, d), bf16),
            pltpu.VMEM((16, d, d), bf16),
            pltpu.VMEM((3, d, d), bf16),
            pltpu.VMEM((rows * cols, 8), f32),
            pltpu.VMEM((mid_count, d), bf16),
            pltpu.VMEM((halo_rows, d), bf16),
            pltpu.VMEM((halo_rows, d), bf16),
            pltpu.VMEM((8 * EDGE, d), bf16),
            pltpu.VMEM((mid_count + 8 * EDGE, d), bf16),
            pltpu.VMEM((8 * EDGE, d), bf16),
            pltpu.VMEM((coarse_padded + 8 * EDGE, d), bf16),
            pltpu.VMEM((8 * mid_count, d), bf16),
            pltpu.VMEM((8 * coarse_padded, d), bf16),
            dma((chunks,)), dma((4,)), dma((chunks,)), dma((chunks,)), dma((24,)), dma((24,)),
        ],
        compiler_params=pltpu.CompilerParams(
            vmem_limit_bytes=60 << 20, collective_id=0, has_side_effects=True
        ),
        name="sweep",
    )(
        fine_nodes.reshape(total, d), mid_nodes.reshape(mid_count, d), coarse, edge_flags,
        proc_weights, bridge_weights, proc_biases, *tables, *levels,
    )
    block = pl.BlockSpec((chunk, d), lambda c: (c, 0))
    refined = pl.pallas_call(
        add_kernel,
        out_shape=jax.ShapeDtypeStruct((total, d), f32),
        grid=(chunks,),
        in_specs=[
            block,
            pl.BlockSpec((chunk // 16, d), lambda c: (c, 0)),
            pl.BlockSpec((chunk, chunk // 16), lambda c: (0, 0)),
        ],
        out_specs=block,
        name="add",
    )(one, spread, jnp.asarray(pool.T, bf16))
    return (refined.reshape(fine_nodes.shape), average.reshape(fine_nodes.shape))


def solution(mesh):
    placed = (
        P(None, "lat", "lon", None),
        P(None, "lat", "lon", None),
        P(None, "lat", "lon", None),
        P(None, "lat", "lon"),
        P(),
        P(),
        P(),
    )
    return jax.shard_map(
        local,
        mesh=mesh,
        in_specs=placed,
        out_specs=(P(None, "lat", "lon", None), P(None, "lat", "lon", None)),
        check_vma=False,
    )
```

profile of v0, /device:TPU:0, one launch (start us, length us, event | category | flops | bytes accessed | tf_op | source)
XLA Modules:
  0.0 56.3 jit_solution(12311942014155128940)
XLA Ops:
  0.6 0.7 %reshape.21 = f32[8,512]{1,0:T(8,128)S(1)} reshape(f32[2,2,2,512]{3,2,1,0:T(2,128)} %param.20) | data formatting | bytes 32768 | tf_op jit(solution)/shard_map/reshape | solution.py:326
  1.4 0.6 %pad.4.coarse_ref = f32[16,512]{1,0:T(8,128)} pad(f32[8,512]{1,0:T(8,128)S(1)} %reshape.21, f32[]{:T(128)} %constant.24.clone.1), padding=0_8x0_0 | pad | bytes 49156 | tf_op jit(solution)/shard_map/jit(_pad)/pad | solution.py:326
  2.0 45.6 %sweep.1 = (f32[2048,512]{1,0:T(8,128)}, bf16[2048,512]{1,0:T(8,128)(2,1)}, bf16[128,512]{1,0:T(8,128)(2,1)}) custom-call(f32[2048,512]{1,0:T(8,128)} %bitcast.4, f32[128,512]{1,0:T(8,128)} %bitcast.7, f32[16,512]{1,0:T(8,128)} %pad.4.coarse_ref, s32[8,32,32]{2,1,0:T(8,128)} %flag_ref.1, bf16[3,4,512,512]{3,2,1,0:T(8,128)(2,1)} %proc_hbm.1, ...), custom_call_target="tpu_custom_call" | custom-call | tf_op jit(solution)/shard_map/sweep/pallas_call | solution.py:331
  47.6 0.0 copy-start
  47.6 7.4 %add.3 = f32[2048,512]{1,0:T(8,128)} custom-call(f32[2048,512]{1,0:T(8,128)} %get-tuple-element.5.one_ref, bf16[128,512]{1,0:T(8,128)(2,1)} %get-tuple-element.6.spread_ref, bf16[256,16]{1,0:T(8,128)(2,1)} %constant.35.clone.table_ref), custom_call_target="tpu_custom_call" | custom-call | tf_op jit(solution)/shard_map/add/pallas_call | solution.py:369
  55.0 0.0 copy-done
  55.0 1.3 %copy.21 = bf16[2,32,32,512]{3,2,1,0:T(8,128)(2,1)} copy(bf16[2,32,32,512]{3,2,1,0:T(8,128)(2,1)S(1)} %bitcast.6) | data formatting | bytes 4194304
Async XLA Ops:
  47.6 7.4 %copy-start = (bf16[2048,512]{1,0:T(8,128)(2,1)S(1)}, bf16[2048,512]{1,0:T(8,128)(2,1)}, u32[]{:S(2)}) copy-start(bf16[2048,512]{1,0:T(8,128)(2,1)} %get-tuple-element.7) | copy-start | bytes 6291460
where the time goes:
time: 56.7 us; the launch traced here: 56.3 us
  Pallas kernels  53 us (93%)
  local copies, waits for them, and re-layouts  2.68 us (5%)
  between operations  0.65 us (1%)
    pallas_call x1, Pallas kernels, local(): pl.pallas_call(functools.partial(sweep_kernel, (samples, rows, cols, d, s...  45.6 us
    pallas_call x1, Pallas kernels, local(): pl.pallas_call(add_kernel, out_shape=jax.ShapeDtypeStruct((total, d), f32...  7.39 us
    unnamed x3, local copies, waits for them, and re-layouts  1.32 us

commit v1 on v0

--- a/solution.py
+++ b/solution.py
@@ -271,7 +271,15 @@
     mid_zero = mid_ref[...] + silu(mm(pool_buf[...], w[12]))
     mid_one = small_pass(1, mid_zero, mid_dims, pick_mid, gather_mid, mid_send, mid_full, mid_hidden)
     small = (mm(pool_mid[...], mid_one.astype(bf16)) * (1 / 16)).astype(bf16)
-    coarse_zero = coarse_ref[...] + silu(mm(small, w[13]))
+    coarse_zero = silu(mm(small, w[13]))
+    row = lax.broadcasted_iota(jnp.int32, coarse_zero.shape, 0)
+    nodes = jnp.zeros(coarse_zero.shape, f32)
+    _, coarse_rows, coarse_cols = coarse_dims
+    for n in range(int(np.prod(coarse_dims))):
+        b, i = divmod(n // coarse_cols, coarse_rows)
+        j = n % coarse_cols
+        nodes = jnp.where(row == n, jnp.broadcast_to(coarse_ref[b, i, j : j + 1, :], nodes.shape), nodes)
+    coarse_zero = coarse_zero + nodes
     coarse_one = small_pass(
         2, coarse_zero, coarse_dims, pick_coarse, gather_coarse, coarse_send, coarse_full, coarse_hidden
     )
@@ -297,7 +305,7 @@
 ):
     samples, rows, cols, d = fine_nodes.shape
     mid_dims, coarse_dims = mid_nodes.shape[:3], coarse_nodes.shape[:3]
-    step = 8
+    step = 16
     chunk = step * cols
     total = samples * rows * cols
     chunks = total // chunk
@@ -323,7 +331,6 @@
         pick_mid, gather_mid, pick_coarse, gather_coarse,
         jnp.asarray(pool_mid, bf16), jnp.asarray(pool_mid.T, bf16),
     ]
-    coarse = jnp.pad(coarse_nodes.reshape(coarse_count, d), ((0, coarse_padded - coarse_count), (0, 0)))
     halo_rows = 2 * samples * (rows + cols) + 4 * EDGE
     vmem = pl.BlockSpec(memory_space=pltpu.VMEM)
     anywhere = pl.BlockSpec(memory_space=pl.ANY)
@@ -362,7 +369,7 @@
         ),
         name="sweep",
     )(
-        fine_nodes.reshape(total, d), mid_nodes.reshape(mid_count, d), coarse, edge_flags,
+        fine_nodes.reshape(total, d), mid_nodes.reshape(mid_count, d), coarse_nodes, edge_flags,
         proc_weights, bridge_weights, proc_biases, *tables, *levels,
     )
     block = pl.BlockSpec((chunk, d), lambda c: (c, 0))

time: 56.7 us -> 49.9 us (0.88)
  Pallas kernels: 53 us -> 47.8 us
  local copies, waits for them, and re-layouts: 2.68 us -> 1.32 us
    pallas_call x1, Pallas kernels: 45.6 us -> 42.5 us  [local(): pl.pallas_call(functools.partial(sweep_kernel, (samples, rows, cols, d, s...]
    pallas_call x1, Pallas kernels: 7.39 us -> 5.27 us  [local(): pl.pallas_call(add_kernel, out_shape=jax.ShapeDtypeStruct((total, d), f32...]
    reshape x1 -> x0, local copies, waits for them, and re-layouts: 0.73 us -> none  [local(): coarse_nodes.reshape(coarse_count, d)]
    pad x1 -> x0, local copies, waits for them, and re-layouts: 0.62 us -> none  [local(): jnp.pad(coarse_nodes.reshape(coarse_count, d), ((0, coarse_padded - coars...]
where the time goes in v1:
time: 49.9 us; the launch traced here: 49.7 us
  Pallas kernels  47.8 us (96%)
  local copies, waits for them, and re-layouts  1.32 us (3%)
  between operations  0.65 us (1%)
    pallas_call x1, Pallas kernels, local(): pl.pallas_call(functools.partial(sweep_kernel, (samples, rows, cols, d, s...  42.5 us
    pallas_call x1, Pallas kernels, local(): pl.pallas_call(add_kernel, out_shape=jax.ShapeDtypeStruct((total, d), f32...  5.27 us
    unnamed x3, local copies, waits for them, and re-layouts  1.32 us

profile of v1, /device:TPU:0, one launch (start us, length us, event | category | flops | bytes accessed | tf_op | source)
XLA Modules:
  0.0 49.7 jit_solution(2100777888621488624)
XLA Ops:
  0.6 42.5 %sweep.1 = (f32[2048,512]{1,0:T(8,128)}, bf16[2048,512]{1,0:T(8,128)(2,1)}, bf16[128,512]{1,0:T(8,128)(2,1)}) custom-call(f32[2048,512]{1,0:T(8,128)} %bitcast.4, f32[128,512]{1,0:T(8,128)} %bitcast.7, f32[2,2,2,512]{3,2,1,0:T(2,128)} %coarse_ref.1, s32[8,32,32]{2,1,0:T(8,128)} %flag_ref.1, bf16[3,4,512,512]{3,2,1,0:T(8,128)(2,1)} %proc_hbm.1, ...), custom_call_target="tpu_custom_call" | custom-call | tf_op jit(solution)/shard_map/sweep/pallas_call | solution.py:338
  43.1 0.0 copy-start
  43.1 5.3 %add.1 = f32[2048,512]{1,0:T(8,128)} custom-call(f32[2048,512]{1,0:T(8,128)} %get-tuple-element.5.one_ref, bf16[128,512]{1,0:T(8,128)(2,1)} %get-tuple-element.6.spread_ref, bf16[512,32]{1,0:T(8,128)(2,1)} %constant.32.clone.table_ref), custom_call_target="tpu_custom_call" | custom-call | tf_op jit(solution)/shard_map/add/pallas_call | solution.py:376
  48.4 0.0 copy-done
  48.4 1.3 %copy.21 = bf16[2,32,32,512]{3,2,1,0:T(8,128)(2,1)} copy(bf16[2,32,32,512]{3,2,1,0:T(8,128)(2,1)S(1)} %bitcast.6) | data formatting | bytes 4194304
Async XLA Ops:
  43.1 5.3 %copy-start = (bf16[2048,512]{1,0:T(8,128)(2,1)S(1)}, bf16[2048,512]{1,0:T(8,128)(2,1)}, u32[]{:S(2)}) copy-start(bf16[2048,512]{1,0:T(8,128)(2,1)} %get-tuple-element.7) | copy-start | bytes 6291460

commit v2 on v1

--- a/solution.py
+++ b/solution.py
@@ -296,8 +296,25 @@
     lax.fori_loop(0, chunks, finish, 0)
 
 
-def add_kernel(one_ref, spread_ref, table_ref, out_ref):
-    out_ref[...] = one_ref[...] + mm(table_ref[...], spread_ref[...])
+def add_kernel(one_hbm, spread_ref, table_ref, out_hbm, buf, in_sems, out_sems):
+    chunk, small = table_ref.shape
+    chunks = buf.shape[0] // chunk
+    windows = [pl.ds(c * chunk, chunk) for c in range(chunks)]
+    loads = [
+        pltpu.make_async_copy(one_hbm.at[w], buf.at[w], in_sems.at[c]) for c, w in enumerate(windows)
+    ]
+    stores = [
+        pltpu.make_async_copy(buf.at[w], out_hbm.at[w], out_sems.at[c]) for c, w in enumerate(windows)
+    ]
+    for load in loads:
+        load.start()
+    for c, w in enumerate(windows):
+        term = mm(table_ref[...], spread_ref[c * small : (c + 1) * small, :])
+        loads[c].wait()
+        buf[w, :] = buf[w, :] + term
+        stores[c].start()
+    for store in stores:
+        store.wait()
 
 
 def local(
@@ -372,17 +389,13 @@
         fine_nodes.reshape(total, d), mid_nodes.reshape(mid_count, d), coarse_nodes, edge_flags,
         proc_weights, bridge_weights, proc_biases, *tables, *levels,
     )
-    block = pl.BlockSpec((chunk, d), lambda c: (c, 0))
     refined = pl.pallas_call(
         add_kernel,
         out_shape=jax.ShapeDtypeStruct((total, d), f32),
-        grid=(chunks,),
-        in_specs=[
-            block,
-            pl.BlockSpec((chunk // 16, d), lambda c: (c, 0)),
-            pl.BlockSpec((chunk, chunk // 16), lambda c: (0, 0)),
-        ],
-        out_specs=block,
+        in_specs=[anywhere, vmem, vmem],
+        out_specs=anywhere,
+        scratch_shapes=[pltpu.VMEM((total, d), f32), dma((chunks,)), dma((chunks,))],
+        compiler_params=pltpu.CompilerParams(vmem_limit_bytes=60 << 20),
         name="add",
     )(one, spread, jnp.asarray(pool.T, bf16))
     return (refined.reshape(fine_nodes.shape), average.reshape(fine_nodes.shape))

time: 49.9 us -> 49.4 us (0.990)
  Pallas kernels: 47.8 us -> 47.2 us
    pallas_call x1, Pallas kernels: 5.27 us -> 4.71 us  [local(): pl.pallas_call(add_kernel, out_shape=jax.ShapeDtypeStruct((total, d), f32...]
where the time goes in v2:
time: 49.4 us; the launch traced here: 49.2 us
  Pallas kernels  47.2 us (96%)
  local copies, waits for them, and re-layouts  1.33 us (3%)
  between operations  0.66 us (1%)
    pallas_call x1, Pallas kernels, local(): pl.pallas_call(functools.partial(sweep_kernel, (samples, rows, cols, d, s...  42.5 us
    pallas_call x1, Pallas kernels, local(): pl.pallas_call(add_kernel, out_shape=jax.ShapeDtypeStruct((total, d), f32...  4.71 us
    unnamed x3, local copies, waits for them, and re-layouts  1.33 us

profile of v2, /device:TPU:0, one launch (start us, length us, event | category | flops | bytes accessed | tf_op | source)
XLA Modules:
  0.0 49.2 jit_solution(135876808539817926)
XLA Ops:
  0.6 42.5 %sweep.1 = (f32[2048,512]{1,0:T(8,128)}, bf16[2048,512]{1,0:T(8,128)(2,1)}, bf16[128,512]{1,0:T(8,128)(2,1)}) custom-call(f32[2048,512]{1,0:T(8,128)} %bitcast.4, f32[128,512]{1,0:T(8,128)} %bitcast.7, f32[2,2,2,512]{3,2,1,0:T(2,128)} %coarse_ref.1, s32[8,32,32]{2,1,0:T(8,128)} %flag_ref.1, bf16[3,4,512,512]{3,2,1,0:T(8,128)(2,1)} %proc_hbm.1, ...), custom_call_target="tpu_custom_call" | custom-call | tf_op jit(solution)/shard_map/sweep/pallas_call | solution.py:355
  43.1 0.0 copy-start
  43.1 4.7 %add.1 = f32[2048,512]{1,0:T(8,128)} custom-call(f32[2048,512]{1,0:T(8,128)} %get-tuple-element.5.one_hbm, bf16[128,512]{1,0:T(8,128)(2,1)} %get-tuple-element.6.spread_ref, bf16[512,32]{1,0:T(8,128)(2,1)} %constant.32.clone.table_ref), custom_call_target="tpu_custom_call" | custom-call | tf_op jit(solution)/shard_map/add/pallas_call | solution.py:392
  47.8 0.0 copy-done
  47.9 1.3 %copy.21 = bf16[2,32,32,512]{3,2,1,0:T(8,128)(2,1)} copy(bf16[2,32,32,512]{3,2,1,0:T(8,128)(2,1)S(1)} %bitcast.6) | data formatting | bytes 4194304
Async XLA Ops:
  43.1 4.7 %copy-start = (bf16[2048,512]{1,0:T(8,128)(2,1)S(1)}, bf16[2048,512]{1,0:T(8,128)(2,1)}, u32[]{:S(2)}) copy-start(bf16[2048,512]{1,0:T(8,128)(2,1)} %get-tuple-element.7) | copy-start | bytes 6291460
